TPU v7x, 32 devices: a whole 2x2x4 slice. The times are simulated.
32 devices in a mesh: row: 4 (over y, core), col: 8 (over z, x).
Axes of the slice: x: 2, y: 2, z: 4, core: 2. Of those that a mesh axis runs over, the one named last changes fastest.
Arguments:
- inverse: float32 [16384, 16384], P('row', 'col'), may hold values from -6 to 6
- front_blocks: int32 [2, 16], replicated, may hold values from 0 to 63, as said below
- panels: float32 [2, 4096, 256], P(None, 'row'), may hold values from -0.09375 to 0.09375
- diag_terms: float32 [2, 256, 256], replicated, may hold values from -6 to 6
- bounds: int32 [2, 4], replicated, may hold values from 1 to 128, 256 in all within a row
Outputs:
- border: float32 [2, 4096, 256], P(None, ('row', 'col'))
- diag_block: float32 [2, 256, 256], replicated
Inputs may be any that keep to these rules, and one draw needn't show every extreme that they name: `front_blocks`: each row names 16 distinct blocks. Positions 4 r to 4 r + 3 name blocks of four different groups of 16 consecutive blocks, and every such group is named at exactly four positions, of four different r. Positions 2 o and 2 o + 1 name blocks of two different groups of 8 consecutive blocks, and every such group is named at exactly two positions, of two different o.
All inputs are finite; a program needn't handle non-finite values.
Results may differ from a plain program's by a relative error of at most 0.0001.
Values sent between devices are 32-bit elements; how exact they have to be, the bound alone decides.
A program may use at most 128 MiB of HBM per device.

v0:
```python
import jax
import jax.numpy as jnp
from jax import lax
from jax.sharding import PartitionSpec as P

BS = 256


def body(inverse, front_blocks, panels, diag_terms, bounds):
    n_row = lax.axis_size("row")
    n_col = lax.axis_size("col")
    row_index = lax.axis_index("row")
    col_index = lax.axis_index("col")
    rows_loc, cols_loc = inverse.shape
    row_group = rows_loc // BS
    col_group = cols_loc // BS
    list_length = front_blocks.shape[1]
    per_owner = list_length // n_row
    highest = lax.Precision.HIGHEST
    borders = []
    diagonals = []
    for front_index in range(2):
        front_list = front_blocks[front_index]
        own_blocks = lax.dynamic_slice_in_dim(front_list, row_index * per_owner, per_owner)
        w_loc = panels[front_index]
        panel_width = w_loc.shape[1]
        w_pieces = w_loc.reshape(per_owner, BS, panel_width)
        targets = col_index * col_group + jnp.arange(col_group, dtype=jnp.int32)
        picker = (own_blocks[None, :] == targets[:, None]).astype(jnp.float32)
        own_piece = jnp.einsum("ki,iab->ab", picker, w_pieces, precision=highest)
        slot_rows = lax.all_gather(own_piece, "row", axis=0, tiled=True).reshape(
            n_row, BS, panel_width
        )
        owners = front_list.reshape(n_row, per_owner)
        placer = jnp.sum((owners[None, :, :] == targets[:, None, None]).astype(jnp.float32), axis=2)
        w_tilde = jnp.einsum("ks,sab->kab", placer, slot_rows, precision=highest).reshape(
            cols_loc, panel_width
        )
        dest_lists = front_list.reshape(n_row, per_owner)
        local_ids = row_index * row_group + jnp.arange(row_group, dtype=jnp.int32)
        share_rows = per_owner * BS // n_col
        full_rows = jnp.dot(inverse, w_tilde, precision=highest)
        quarters = BS // share_rows
        full_pieces = full_rows.reshape(row_group, quarters, share_rows, panel_width)
        first_rows = jnp.arange(n_col, dtype=jnp.int32) * share_rows
        dest_block = dest_lists[:, first_rows // BS]
        block_pick = (dest_block.T[:, :, None] == local_ids[None, None, :]).astype(jnp.float32)
        quarter_pick = (
            (first_rows % BS // share_rows)[:, None]
            == jnp.arange(quarters, dtype=jnp.int32)[None, :]
        ).astype(jnp.float32)
        sectioned = jnp.einsum("cq,kqap->ckap", quarter_pick, full_pieces, precision=highest)
        ordered = jnp.einsum("cdk,ckap->cdap", block_pick, sectioned, precision=highest)
        ordered = ordered.reshape(n_col * n_row * share_rows, panel_width)
        reduced = lax.psum_scatter(ordered, "col", scatter_dimension=0, tiled=True)
        received = lax.all_to_all(
            reduced.reshape(n_row, share_rows, panel_width),
            "row",
            split_axis=0,
            concat_axis=0,
            tiled=True,
        )
        product = jnp.sum(received, axis=0)
        w_mine = lax.dynamic_slice_in_dim(w_loc, col_index * share_rows, share_rows, 0)
        own_term = jnp.dot(w_mine.T, product, precision=highest)
        summed_total = lax.psum(own_term, ("row", "col"))
        node_ends = jnp.cumsum(bounds[front_index])
        columns = jnp.arange(panel_width, dtype=jnp.int32)
        node_ids = jnp.sum((columns[:, None] >= node_ends[None, :]).astype(jnp.int32), axis=1)
        same_node = (node_ids[:, None] == node_ids[None, :]).astype(jnp.float32)
        borders.append(-product)
        diagonals.append(same_node * (diag_terms[front_index] + summed_total))
    return (jnp.stack(borders), jnp.stack(diagonals))


def solution(mesh):
    placed = (P("row", "col"), P(), P(None, "row", None), P(), P())
    return jax.shard_map(
        body,
        mesh=mesh,
        in_specs=placed,
        out_specs=(P(None, ("row", "col"), None), P()),
        check_vma=False,
    )
```

profile of v0, /device:TPU:0, one launch (start us, length us, event | category | flops | bytes accessed | tf_op | source)
XLA Modules:
  0.0 484.4 jit_solution(6554460476007873666)
XLA Ops:
  7.2 0.8 slice_reduce_fusion.1
  8.0 1.7 fusion.46
  9.7 0.1 fusion.38
  9.8 0.2 convert_reduce_fusion.5
  10.0 2.3 fusion.6
  12.3 0.7 copy.51
  13.1 0.0 all-gather.5.cloned.1.call-start
  13.1 2.3 fusion.4
  15.5 0.7 copy.50
  16.2 0.0 reduce-scatter.3.cloned.1.call-start
  16.3 0.1 reshape_squeeze.12
  16.4 0.1 reshape_squeeze.14
  16.5 0.1 copy.17
  16.5 0.1 convert_reduce_fusion.1
  16.7 0.6 gather_fusion
  17.2 15.4 %all-gather.3.cloned.1.call-done = f32[1024,256]{1,0:T(8,128)} async-done(((f32[256,256]{1,0:T(8,128)}), f32[1024,256]{1,0:T(8,128)}) %all-gather.3.cloned.1.call-update) | async-done | bytes 1048592 | tf_op jit(solution)/shard_map/all_gather | solution.py:31
  32.6 4.0 fusion.10
  36.7 0.7 copy.19
  37.4 58.5 %convolution_bitcast_fusion.1 = f32[4096,256]{0,1:T(8,128)} fusion(f32[2048,256]{1,0:T(8,128)S(1)} %bitcast.104, f32[4096,2048]{1,0:T(8,128)} %param.5), kind=kOutput, calls=%fused_computation.7 | convolution fusion | flops 25769803776 | bytes 39845888 | tf_op jit(solution)/shard_map/dot_general | solution.py:42
  95.9 6.6 %reshape.215 = f32[16,2,128,256]{2,1,0,3:T(2,128)} reshape(f32[4096,256]{0,1:T(8,128)} %convolution_bitcast_fusion.1) | data formatting | bytes 8388608 | tf_op jit(solution)/shard_map/reshape | solution.py:44
  102.5 9.3 %copy.20 = f32[16,2,128,256]{3,1,2,0:T(2,128)} copy(f32[16,2,128,256]{2,1,0,3:T(2,128)} %reshape.215) | data formatting | bytes 8388608 | tf_op jit(solution)/shard_map/reshape | solution.py:44
  111.8 11.7 %fusion.34 = f32[8,16,128,256]{3,0,2,1:T(8,128)S(1)} fusion(f32[16,2,128,256]{3,1,2,0:T(2,128)} %copy.20, s32[8]{0:T(128)S(1)} %and_select_fusion), kind=kOutput, calls=%fused_computation.58 | convolution fusion | flops 100663312 | bytes 20971552 | tf_op jit(solution)/shard_map/cq,kqap->ckap/dot_general | solution.py:52
  123.5 12.2 %fusion.2 = f32[8,4,128,256]{3,1,2,0:T(4,128)S(1)} fusion(f32[8,16,128,256]{3,0,2,1:T(8,128)S(1)} %fusion.34, s32[16]{0:T(128)S(1)} %iota_add_fusion.1, s32[8,4]{1,0:T(8,128)S(1)} %gather_fusion), kind=kOutput, calls=%fused_computation.4 | convolution fusion | flops 201327104 | bytes 20971712 | tf_op jit(solution)/shard_map/cdk,ckap->cdap/dot_general | solution.py:53
  135.7 2.7 copy.22
  138.4 0.0 reduce-scatter.5.cloned.1.call-start
  138.5 0.1 copy.23
  138.5 0.6 gather_fusion.1
  139.1 4.0 fusion.8
  143.2 0.7 copy.25
  143.8 58.8 %convolution_bitcast_fusion = f32[4096,256]{0,1:T(8,128)} fusion(f32[2048,256]{1,0:T(8,128)S(1)} %bitcast.105, f32[4096,2048]{1,0:T(8,128)} %param.5), kind=kOutput, calls=%fused_computation.6 | convolution fusion | flops 25769803776 | bytes 39845888 | tf_op jit(solution)/shard_map/dot_general | solution.py:42
  202.6 6.7 %reshape.220 = f32[16,2,128,256]{2,1,0,3:T(2,128)} reshape(f32[4096,256]{0,1:T(8,128)} %convolution_bitcast_fusion) | data formatting | bytes 8388608 | tf_op jit(solution)/shard_map/reshape | solution.py:44
  209.3 9.3 %copy.26 = f32[16,2,128,256]{3,1,2,0:T(2,128)} copy(f32[16,2,128,256]{2,1,0,3:T(2,128)} %reshape.220) | data formatting | bytes 8388608 | tf_op jit(solution)/shard_map/reshape | solution.py:44
  218.6 11.7 %fusion.32 = f32[8,16,128,256]{3,0,2,1:T(8,128)S(1)} fusion(f32[16,2,128,256]{3,1,2,0:T(2,128)} %copy.26, s32[8]{0:T(128)S(1)} %and_select_fusion), kind=kOutput, calls=%fused_computation.56 | convolution fusion | flops 100663312 | bytes 20971552 | tf_op jit(solution)/shard_map/cq,kqap->ckap/dot_general | solution.py:52
  230.3 12.2 %fusion = f32[8,4,128,256]{3,1,2,0:T(4,128)S(1)} fusion(f32[8,16,128,256]{3,0,2,1:T(8,128)S(1)} %fusion.32, s32[8,4]{1,0:T(8,128)S(1)} %gather_fusion.1, s32[16]{0:T(128)S(1)} %iota_add_fusion.1), kind=kOutput, calls=%fused_computation.2 | convolution fusion | flops 201327104 | bytes 20971712 | tf_op jit(solution)/shard_map/cdk,ckap->cdap/dot_general | solution.py:53
  242.5 2.7 copy.28
  245.3 3.6 all-to-all-start
  248.9 0.2 reduce-window.16
  249.1 0.2 reduce-window.17
  249.3 0.1 convert_reduce_fusion.2
  249.4 84.5 %reduce-scatter.5.cloned.1.call-done = f32[512,256]{1,0:T(8,128)} async-done(((f32[4096,256]{1,0:T(8,128)}), f32[512,256]{1,0:T(8,128)}) %reduce-scatter.5.cloned.1.call-update) | async-done | bytes 524304 | tf_op jit(solution)/shard_map/reduce_scatter | solution.py:55
  333.9 3.5 all-to-all-start.1
  337.5 2.1 fusion.18
  339.5 6.6 %all-to-all-done.1 = f32[4,128,256]{2,1,0:T(8,128)S(1)} async-done(((f32[4,128,256]{2,1,0:T(8,128)}), f32[4,128,256]{2,1,0:T(8,128)S(1)}, u32[]{:S(2)}, u32[]{:S(2)}) %all-to-all-start.1) | async-done | bytes 524320 | tf_op jit(solution)/shard_map/all_to_all | solution.py:56
  346.2 1.1 fusion.16
  347.3 0.7 pad_maximum_fusion.1
  348.1 127.4 %all-reduce.3.cloned.1.call-done = (f32[256,256]{1,0:T(8,128)}, f32[256,256]{1,0:T(8,128)}) async-done(((f32[256,256]{1,0:T(8,128)}, f32[256,256]{1,0:T(8,128)}), (f32[256,256]{1,0:T(8,128)}, f32[256,256]{1,0:T(8,128)})) %all-reduce.3.cloned.1.call-update) | async-done | bytes 524304 | tf_op jit(solution)/shard_map/psum | solution.py:66
  475.5 1.2 fusion.15
  476.7 0.8 pad_maximum_fusion
  (26 shorter events, 0.4 us)
Async XLA Ops:
  7.2 25.5 %all-gather.3.cloned.1.call-start = ((), (), s32[]{:S(2)}) async-start(), calls=%async_computation.4 | async-start | bytes 1310720 | tf_op jit(solution)/shard_map/all_gather | solution.py:31
  9.7 27.7 %copy-start = (f32[1,1024,256]{2,1,0:T(8,128)}, f32[1,1024,256]{2,1,0:T(8,128)S(1)}, u32[]{:S(2)}) copy-start(f32[1,1024,256]{2,1,0:T(8,128)S(1)} %get-tuple-element.10) | copy-start | bytes 3145732
  13.1 126.1 %all-gather.5.cloned.1.call-start = ((), (), s32[]{:S(2)}) async-start(), calls=%async_computation.6 | async-start | bytes 1310720 | tf_op jit(solution)/shard_map/all_gather | solution.py:31
  16.2 229.1 %reduce-scatter.3.cloned.1.call-start = ((), (), s32[]{:S(2)}) async-start(), calls=%async_computation.5 | async-start | bytes 4718592 | tf_op jit(solution)/shard_map/reduce_scatter | solution.py:55
  138.4 195.5 %reduce-scatter.5.cloned.1.call-start = ((), (), s32[]{:S(2)}) async-start(), calls=%async_computation.7 | async-start | bytes 4718592 | tf_op jit(solution)/shard_map/reduce_scatter | solution.py:55
  245.2 3.7 copy-start.2
  245.2 230.3 %copy-start.1 = (f32[2,256,256]{2,1,0:T(8,128)S(1)}, f32[2,256,256]{2,1,0:T(8,128)}, u32[]{:S(2)}) copy-start(f32[2,256,256]{2,1,0:T(8,128)} %param.8) | copy-start | bytes 1572868
  245.3 88.6 %all-to-all-start = ((f32[4,128,256]{2,1,0:T(8,128)}), f32[4,128,256]{2,1,0:T(8,128)S(1)}, u32[]{:S(2)}, u32[]{:S(2)}) async-start(f32[4,128,256]{2,1,0:T(8,128)} %bitcast.112), calls=%async_computation.1 | async-start | bytes 1048576 | tf_op jit(solution)/shard_map/all_to_all | solution.py:56
  333.9 12.3 %all-to-all-start.1 = ((f32[4,128,256]{2,1,0:T(8,128)}), f32[4,128,256]{2,1,0:T(8,128)S(1)}, u32[]{:S(2)}, u32[]{:S(2)}) async-start(f32[4,128,256]{2,1,0:T(8,128)} %bitcast.113), calls=%async_computation.3 | async-start | bytes 1048576 | tf_op jit(solution)/shard_map/all_to_all | solution.py:56
  337.3 138.2 %all-reduce.3.cloned.1.call-start = ((), (), s32[]{:S(2)}) async-start(), calls=%async_computation.8 | async-start | bytes 1048576 | tf_op jit(solution)/shard_map/psum | solution.py:66
Sparse Core Ops, SparseCore 0:
  13.2 19.4 all-gather.2
  34.8 16.6 all-gather.4
  138.5 88.2 reduce-scatter.2
  245.4 88.4 reduce-scatter.4
  347.4 128.0 all-reduce.2
where the time goes:
time: 492 us; the launch traced here: 484 us
  waiting for transfers between devices  234 us (48%)
  matrix products  181 us (37%)
  local copies, waits for them, and re-layouts  44.1 us (9%)
  between operations  14.4 us (3%)
  starting transfers between devices  7.29 us (1%)
    psum x1, waiting for transfers between devices, body(): summed_total = lax.psum(own_term, ('row', 'col'))  127 us
    dot_general x2, matrix products, body(): full_rows = jnp.dot(inverse, w_tilde, precision=highest)  117 us
    reduce_scatter x2, waiting for transfers between devices, body(): reduced = lax.psum_scatter(ordered, 'col', scatter_dimension=0, tiled=True)  84.5 us
    reshape x4, local copies, waits for them, and re-layouts, body(): full_rows.reshape(row_group, quarters, share_rows, panel_width)  31.9 us
    dot_general x2, matrix products, body(): jnp.einsum('cdk,ckap->cdap', block_pick, sectioned, precision=highest)  24.4 us
    dot_general x2, matrix products, body(): jnp.einsum('cq,kqap->ckap', quarter_pick, full_pieces, precision=highest)  23.4 us
    all_gather x2, waiting for transfers between devices, body(): lax.all_gather(own_piece, 'row', axis=0, tiled=True)  15.4 us
  transfers between devices with their start and end apart: 7, of which 4 were waited for; matrix products, arithmetic and copies ran while one was open for 45% of the time, Pallas kernels for 0%

commit v1 on v0

--- a/solution.py
+++ b/solution.py
@@ -63,7 +63,7 @@
         product = jnp.sum(received, axis=0)
         w_mine = lax.dynamic_slice_in_dim(w_loc, col_index * share_rows, share_rows, 0)
         own_term = jnp.dot(w_mine.T, product, precision=highest)
-        summed_total = lax.psum(own_term, ("row", "col"))
+        summed_total = jnp.sum(lax.all_gather(own_term, ("row", "col")), axis=0)
         node_ends = jnp.cumsum(bounds[front_index])
         columns = jnp.arange(panel_width, dtype=jnp.int32)
         node_ids = jnp.sum((columns[:, None] >= node_ends[None, :]).astype(jnp.int32), axis=1)

time: 492 us -> 513 us (1.043)
  blocking collectives: 0 us -> 12.3 us
  other arithmetic: 3.57 us -> 10.5 us
    all_gather x0 -> x2, waiting for transfers between devices: none -> 140 us  [body(): summed_total = jnp.sum(lax.all_gather(own_term, ('row', 'col')), axis=0)]
    psum x1 -> x0, waiting for transfers between devices: 127 us -> none  [body(): summed_total = lax.psum(own_term, ('row', 'col'))]
    all_to_all x0 -> x1, blocking collectives: none -> 12.3 us  [body(): lax.all_to_all(reduced.reshape(n_row, share_rows, panel_width), 'row', sp...]
    reduce_scatter x2, waiting for transfers between devices: 84.5 us -> 74.1 us  [body(): reduced = lax.psum_scatter(ordered, 'col', scatter_dimension=0, tiled=True)]
    reduce_sum x0 -> x2, other arithmetic: none -> 7.91 us  [body(): summed_total = jnp.sum(lax.all_gather(own_term, ('row', 'col')), axis=0)]
  transfers between devices with their start and end apart: 7 -> 7, of which waited for: 4 -> 5; matrix products, arithmetic and copies ran while one was open for 45% -> 45% of each run, Pallas kernels for 0% -> 0%
where the time goes in v1:
time: 513 us; the launch traced here: 505 us
  waiting for transfers between devices  238 us (46%)
  matrix products  181 us (35%)
  local copies, waits for them, and re-layouts  44.1 us (9%)
  between operations  14.8 us (3%)
  blocking collectives  12.3 us (2%)
  other arithmetic  10.5 us (2%)
    all_gather x2, waiting for transfers between devices, body(): summed_total = jnp.sum(lax.all_gather(own_term, ('row', 'col')), axis=0)  140 us
    dot_general x2, matrix products, body(): full_rows = jnp.dot(inverse, w_tilde, precision=highest)  117 us
    reduce_scatter x2, waiting for transfers between devices, body(): reduced = lax.psum_scatter(ordered, 'col', scatter_dimension=0, tiled=True)  74.1 us
    reshape x4, local copies, waits for them, and re-layouts, body(): full_rows.reshape(row_group, quarters, share_rows, panel_width)  31.9 us
    dot_general x2, matrix products, body(): jnp.einsum('cdk,ckap->cdap', block_pick, sectioned, precision=highest)  24.4 us
    dot_general x2, matrix products, body(): jnp.einsum('cq,kqap->ckap', quarter_pick, full_pieces, precision=highest)  23.4 us
    all_gather x2, waiting for transfers between devices, body(): lax.all_gather(own_piece, 'row', axis=0, tiled=True)  15.4 us
    all_to_all x1, blocking collectives, body(): lax.all_to_all(reduced.reshape(n_row, share_rows, panel_width), 'row', sp...  12.3 us
  transfers between devices with their start and end apart: 7, of which 5 were waited for; matrix products, arithmetic and copies ran while one was open for 45% of the time, Pallas kernels for 0%

profile of v1, /device:TPU:0, one launch (start us, length us, event | category | flops | bytes accessed | tf_op | source)
XLA Modules:
  0.0 504.9 jit_solution(9402645380075751152)
XLA Ops:
  7.2 0.8 slice_reduce_fusion.1
  8.0 1.7 fusion.44
  9.8 0.2 convert_reduce_fusion.5
  10.0 2.3 fusion.6
  12.3 0.7 copy.51
  13.1 2.3 fusion.4
  15.5 0.7 copy.50
  16.3 0.1 reshape_squeeze.12
  16.4 0.1 reshape_squeeze.14
  16.5 0.1 copy.17
  16.5 0.1 convert_reduce_fusion.1
  16.7 0.6 gather_fusion
  17.2 15.4 %all-gather.7.cloned.1.call-done = f32[1024,256]{1,0:T(8,128)} async-done(((f32[256,256]{1,0:T(8,128)}), f32[1024,256]{1,0:T(8,128)}) %all-gather.7.cloned.1.call-update) | async-done | bytes 1048592 | tf_op jit(solution)/shard_map/all_gather | solution.py:31
  32.6 4.0 fusion.10
  36.7 0.7 copy.19
  37.4 58.5 %convolution_bitcast_fusion.1 = f32[4096,256]{0,1:T(8,128)} fusion(f32[2048,256]{1,0:T(8,128)S(1)} %bitcast.98, f32[4096,2048]{1,0:T(8,128)} %param.5), kind=kOutput, calls=%fused_computation.7 | convolution fusion | flops 25769803776 | bytes 39845888 | tf_op jit(solution)/shard_map/dot_general | solution.py:42
  95.9 6.6 %reshape.299 = f32[16,2,128,256]{2,1,0,3:T(2,128)} reshape(f32[4096,256]{0,1:T(8,128)} %convolution_bitcast_fusion.1) | data formatting | bytes 8388608 | tf_op jit(solution)/shard_map/reshape | solution.py:44
  102.5 9.3 %copy.20 = f32[16,2,128,256]{3,1,2,0:T(2,128)} copy(f32[16,2,128,256]{2,1,0,3:T(2,128)} %reshape.299) | data formatting | bytes 8388608 | tf_op jit(solution)/shard_map/reshape | solution.py:44
  111.8 11.7 %fusion.32 = f32[8,16,128,256]{3,0,2,1:T(8,128)S(1)} fusion(f32[16,2,128,256]{3,1,2,0:T(2,128)} %copy.20, s32[8]{0:T(128)S(1)} %and_select_fusion), kind=kOutput, calls=%fused_computation.56 | convolution fusion | flops 100663312 | bytes 20971552 | tf_op jit(solution)/shard_map/cq,kqap->ckap/dot_general | solution.py:52
  123.5 12.2 %fusion.2 = f32[8,4,128,256]{3,1,2,0:T(4,128)S(1)} fusion(f32[8,16,128,256]{3,0,2,1:T(8,128)S(1)} %fusion.32, s32[16]{0:T(128)S(1)} %iota_add_fusion.1, s32[8,4]{1,0:T(8,128)S(1)} %gather_fusion), kind=kOutput, calls=%fused_computation.4 | convolution fusion | flops 201327104 | bytes 20971712 | tf_op jit(solution)/shard_map/cdk,ckap->cdap/dot_general | solution.py:53
  135.7 2.7 copy.22
  138.5 0.1 copy.23
  138.5 0.6 gather_fusion.1
  139.1 4.0 fusion.8
  143.2 0.7 copy.25
  143.8 58.8 %convolution_bitcast_fusion = f32[4096,256]{0,1:T(8,128)} fusion(f32[2048,256]{1,0:T(8,128)S(1)} %bitcast.99, f32[4096,2048]{1,0:T(8,128)} %param.5), kind=kOutput, calls=%fused_computation.6 | convolution fusion | flops 25769803776 | bytes 39845888 | tf_op jit(solution)/shard_map/dot_general | solution.py:42
  202.6 6.7 %reshape.304 = f32[16,2,128,256]{2,1,0,3:T(2,128)} reshape(f32[4096,256]{0,1:T(8,128)} %convolution_bitcast_fusion) | data formatting | bytes 8388608 | tf_op jit(solution)/shard_map/reshape | solution.py:44
  209.3 9.3 %copy.26 = f32[16,2,128,256]{3,1,2,0:T(2,128)} copy(f32[16,2,128,256]{2,1,0,3:T(2,128)} %reshape.304) | data formatting | bytes 8388608 | tf_op jit(solution)/shard_map/reshape | solution.py:44
  218.6 11.7 %fusion.30 = f32[8,16,128,256]{3,0,2,1:T(8,128)S(1)} fusion(f32[16,2,128,256]{3,1,2,0:T(2,128)} %copy.26, s32[8]{0:T(128)S(1)} %and_select_fusion), kind=kOutput, calls=%fused_computation.54 | convolution fusion | flops 100663312 | bytes 20971552 | tf_op jit(solution)/shard_map/cq,kqap->ckap/dot_general | solution.py:52
  230.3 12.2 %fusion = f32[8,4,128,256]{3,1,2,0:T(4,128)S(1)} fusion(f32[8,16,128,256]{3,0,2,1:T(8,128)S(1)} %fusion.30, s32[8,4]{1,0:T(8,128)S(1)} %gather_fusion.1, s32[16]{0:T(128)S(1)} %iota_add_fusion.1), kind=kOutput, calls=%fused_computation.2 | convolution fusion | flops 201327104 | bytes 20971712 | tf_op jit(solution)/shard_map/cdk,ckap->cdap/dot_general | solution.py:53
  242.5 2.7 copy.28
  245.3 3.5 all-to-all-start
  248.8 0.3 all-gather.11.cloned.1.call-start
  249.1 8.5 %all-to-all-done = f32[4,128,256]{2,1,0:T(8,128)S(1)} async-done(((f32[4,128,256]{2,1,0:T(8,128)}), f32[4,128,256]{2,1,0:T(8,128)S(1)}, u32[]{:S(2)}, u32[]{:S(2)}) %all-to-all-start) | async-done | bytes 524320 | tf_op jit(solution)/shard_map/all_to_all | solution.py:56
  257.6 2.0 fusion.16
  259.7 74.1 %reduce-scatter.5.cloned.1.call-done = f32[512,256]{1,0:T(8,128)} async-done(((f32[4096,256]{1,0:T(8,128)}), f32[512,256]{1,0:T(8,128)}) %reduce-scatter.5.cloned.1.call-update) | async-done | bytes 524304 | tf_op jit(solution)/shard_map/reduce_scatter | solution.py:55
  333.8 12.3 %all_to_all.10 = f32[4,128,256]{2,1,0:T(8,128)S(1)} all-to-all(f32[4,128,256]{2,1,0:T(8,128)} %bitcast.109), channel_id=1, replica_groups=mesh['row'=4,'col'=8] {'row'}, dimensions={0} | all-to-all | bytes 1048576 | tf_op jit(solution)/shard_map/all_to_all | solution.py:56
  346.1 1.1 fusion.14
  347.2 0.2 reduce-window.16
  347.4 0.2 reduce-window.17
  347.6 0.1 convert_reduce_fusion.2
  347.7 0.7 pad_maximum_fusion.1
  348.4 65.6 %all-gather.11.cloned.1.call-done = f32[8192,256]{1,0:T(8,128)} async-done(((f32[256,256]{1,0:T(8,128)}), f32[8192,256]{1,0:T(8,128)}) %all-gather.11.cloned.1.call-update) | async-done | bytes 8388624 | tf_op jit(solution)/shard_map/all_gather | solution.py:66
  414.0 3.9 reduce_sum.101
  417.9 74.7 %all-gather.13.cloned.1.call-done = f32[8192,256]{1,0:T(8,128)} async-done(((f32[256,256]{1,0:T(8,128)}), f32[8192,256]{1,0:T(8,128)}) %all-gather.13.cloned.1.call-update) | async-done | bytes 8388624 | tf_op jit(solution)/shard_map/all_gather | solution.py:66
  492.6 4.0 reduce_sum.104
  496.6 0.1 fusion.13
  496.7 0.8 pad_maximum_fusion
  (30 shorter events, 0.6 us)
Async XLA Ops:
  7.2 25.5 %all-gather.7.cloned.1.call-start = ((), (), s32[]{:S(2)}) async-start(), calls=%async_computation.4 | async-start | bytes 1310720 | tf_op jit(solution)/shard_map/all_gather | solution.py:31
  9.7 27.7 %copy-start = (f32[1,1024,256]{2,1,0:T(8,128)}, f32[1,1024,256]{2,1,0:T(8,128)S(1)}, u32[]{:S(2)}) copy-start(f32[1,1024,256]{2,1,0:T(8,128)S(1)} %get-tuple-element.8) | copy-start | bytes 3145732
  13.1 126.1 %all-gather.9.cloned.1.call-start = ((), (), s32[]{:S(2)}) async-start(), calls=%async_computation.6 | async-start | bytes 1310720 | tf_op jit(solution)/shard_map/all_gather | solution.py:31
  16.2 229.1 %reduce-scatter.3.cloned.1.call-start = ((), (), s32[]{:S(2)}) async-start(), calls=%async_computation.5 | async-start | bytes 4718592 | tf_op jit(solution)/shard_map/reduce_scatter | solution.py:55
  138.4 195.4 %reduce-scatter.5.cloned.1.call-start = ((), (), s32[]{:S(2)}) async-start(), calls=%async_computation.7 | async-start | bytes 4718592 | tf_op jit(solution)/shard_map/reduce_scatter | solution.py:55
  245.2 102.0 %copy-start.2 = (s32[2,4]{1,0:T(2,128)S(1)}, s32[2,4]{1,0:T(2,128)}, u32[]{:S(2)}) copy-start(s32[2,4]{1,0:T(2,128)} %param.9) | copy-start | bytes 100
  245.3 12.3 %all-to-all-start = ((f32[4,128,256]{2,1,0:T(8,128)}), f32[4,128,256]{2,1,0:T(8,128)S(1)}, u32[]{:S(2)}, u32[]{:S(2)}) async-start(f32[4,128,256]{2,1,0:T(8,128)} %bitcast.108), calls=%async_computation.1 | async-start | bytes 1048576 | tf_op jit(solution)/shard_map/all_to_all | solution.py:56
  248.8 165.2 %all-gather.11.cloned.1.call-start = ((), (), s32[]{:S(2)}) async-start(), calls=%async_computation.8 | async-start | bytes 8650752 | tf_op jit(solution)/shard_map/all_gather | solution.py:66
  259.7 232.9 %all-gather.13.cloned.1.call-start = ((), (), s32[]{:S(2)}) async-start(), calls=%async_computation.9 | async-start | bytes 8650752 | tf_op jit(solution)/shard_map/all_gather | solution.py:66
  492.6 4.0 copy-start.1
Sparse Core Ops, SparseCore 0:
  13.2 19.4 all-gather.6
  34.8 16.6 all-gather.8
  138.5 88.2 reduce-scatter.2
  245.4 88.3 reduce-scatter.4
  337.2 76.7 all-gather.10
  416.9 75.6 all-gather.12
